TPU v7x, 512 devices: a whole 4x8x8 slice. The times are simulated.
512 devices in a mesh: panel: 2 (over y_lo), lon: 16 (over z, core), lat: 16 (over y_hi, x).
Axes of the slice: x: 4, y: 8 (y_hi: 4, y_lo: 2; y = y_hi * 2 + y_lo), z: 8, core: 2. Of those that a mesh axis runs over, the one named last changes fastest.
Arguments:
- pressure: float32 [2, 256, 512, 128], P('panel', 'lat', 'lon'), may hold values from -6 to 6
- porosity: float32 [2, 256, 512, 128], P('panel', 'lat', 'lon'), may hold values from 0.5 to 2
- source: float32 [2, 256, 512, 128], P('panel', 'lat', 'lon'), may hold values from -6 to 6
- bulk: float32 [2, 256, 512, 128], P('panel', 'lat', 'lon'), may hold values from 0.5 to 2
- lat_codes: int32 [2, 2, 2, 512], P('panel', None, None, 'lon'), may hold values from 0 to 8158, as said below
- lat_weights: float32 [2, 4, 2, 2, 512], P('panel', None, None, None, 'lon'), may hold values from 0 to 1, as said below
- lon_codes: int32 [2, 2, 2, 256], P('panel', None, None, 'lat'), may hold values from 0 to 8174, as said below
- lon_weights: float32 [2, 4, 2, 2, 256], P('panel', None, None, None, 'lat'), may hold values from 0 to 1, as said below
Outputs:
- pressure_out: float32 [2, 256, 512, 128], P('panel', 'lat', 'lon')
- porosity_out: float32 [2, 256, 512, 128], P('panel', 'lat', 'lon')
Inputs may be any that keep to these rules, and one draw needn't show every extreme that they name: `lat_codes`: an intersection map of the shell, which may differ from draw to draw: code = a * 32 + c with a < 255 a latitude of the whole panel and c < 31 an offset inside the longitude block of the ghost cell. `lon_codes`: an intersection map of the shell, which may differ from draw to draw: code = b * 16 + r with b < 511 a longitude of the whole panel and r < 15 an offset inside the latitude block of the ghost cell. `lat_weights`: the four weights of a ghost cell are non-negative and sum to one. `lon_weights`: the four weights of a ghost cell are non-negative and sum to one.
All inputs are finite; a program needn't handle non-finite values.
Results may differ from a plain program's by a relative error of at most 0.0003.
Values sent between devices are 32-bit elements; how exact they have to be, the bound alone decides.
A program may use at most 64 MiB of HBM per device.

v0:
```python
import jax
import jax.numpy as jnp
from jax import lax
from jax.sharding import PartitionSpec as P

SWEEPS = 3
stencil_offsets = ((0, 0), (0, 1), (1, 0), (1, 1))
radial_weight = 0.25
buoyancy = 0.5
time_step = 0.04


def padded_2(cells, sides, width):
    for axis, dim in sides:
        count = lax.axis_size(axis)
        ends = count - 1
        head = lax.slice_in_dim(cells, 0, width, axis=dim)
        tail = lax.slice_in_dim(cells, cells.shape[dim] - width, cells.shape[dim], axis=dim)
        cells = jnp.concatenate(
            [
                lax.ppermute(tail, axis, [(i, (i + 1) % count) for i in range(ends)]),
                cells,
                lax.ppermute(head, axis, [((i + 1) % count, i) for i in range(ends)]),
            ],
            axis=dim,
        )
    return cells


def swapped(block, axis, distance):
    count = lax.axis_size(axis)
    route = []
    for low in range(count):
        high = low | 1 << distance
        if high != low and high < count:
            route += [(low, high), (high, low)]
    return lax.ppermute(block, axis, route)


def pad_last(values, before, after):
    widths = [(0, 0)] * (values.ndim - 1) + [(before, after)]
    return jnp.pad(values, widths)


def rim_terms(field, lat_codes, lat_weights, lon_codes, lon_weights, width):
    rows_dev, cols_dev, levels = field.shape
    first_row = lax.axis_index("lat") * rows_dev
    first_col = lax.axis_index("lon") * cols_dev
    chosen = lat_codes[:, :width]
    rows_at = chosen // cols_dev - first_row
    cols_at = chosen % cols_dev
    lat_total = jnp.zeros(chosen.shape + (levels,), jnp.float32)
    for corner, (row_step, col_step) in enumerate(stencil_offsets):
        target = rows_at + row_step
        inside = (target >= 0) & (target < rows_dev)
        picked = field[jnp.clip(target, 0, rows_dev - 1), cols_at + col_step]
        lat_total = (
            lat_total + jnp.where(inside, lat_weights[corner, :, :width], 0.0)[..., None] * picked
        )
    chosen = lon_codes[:, :width]
    cols_at = chosen // rows_dev - first_col
    rows_at = chosen % rows_dev
    lon_total = jnp.zeros(chosen.shape + (levels,), jnp.float32)
    for corner, (row_step, col_step) in enumerate(stencil_offsets):
        target = cols_at + col_step
        inside = (target >= 0) & (target < cols_dev)
        picked = field[rows_at + row_step, jnp.clip(target, 0, cols_dev - 1)]
        lon_total = (
            lon_total + jnp.where(inside, lon_weights[corner, :, :width], 0.0)[..., None] * picked
        )
    return (lat_total, lon_total)


def surround(field, width, lat_codes, lat_weights, lon_codes, lon_weights):
    rows_dev, cols_dev, levels = field.shape
    padded = padded_2(field, (("lat", 0), ("lon", 1)), width)
    lat_terms, lon_terms = rim_terms(field, lat_codes, lat_weights, lon_codes, lon_weights, width)
    lat_summed = lax.psum(lat_terms, "lat")
    lon_summed = lax.psum(lon_terms, "lon")
    arrived = swapped(jnp.concatenate([lat_summed, lon_summed], axis=2), "panel", 0)
    lat_rim = arrived[:, :, :cols_dev]
    lon_rim = arrived[:, :, cols_dev:]
    lat_index = lax.axis_index("lat")
    lon_index = lax.axis_index("lon")
    last_lat = lax.axis_size("lat") - 1
    last_lon = lax.axis_size("lon") - 1
    north = jnp.where(lat_index == 0, lat_rim[0][::-1], padded[:width, width : width + cols_dev])
    padded = padded.at[:width, width : width + cols_dev].set(north)
    south = jnp.where(
        lat_index == last_lat, lat_rim[1], padded[width + rows_dev :, width : width + cols_dev]
    )
    padded = padded.at[width + rows_dev :, width : width + cols_dev].set(south)
    west = jnp.where(
        lon_index == 0,
        jnp.moveaxis(lon_rim[0][::-1], 0, 1),
        padded[width : width + rows_dev, :width],
    )
    padded = padded.at[width : width + rows_dev, :width].set(west)
    east = jnp.where(
        lon_index == last_lon,
        jnp.moveaxis(lon_rim[1], 0, 1),
        padded[width : width + rows_dev, width + cols_dev :],
    )
    padded = padded.at[width : width + rows_dev, width + cols_dev :].set(east)
    return padded


def face_terms(mobility):
    lat_face = 0.5 * (mobility[..., :-1, 1:-1, :] + mobility[..., 1:, 1:-1, :])
    lon_face = 0.5 * (mobility[..., 1:-1, :-1, :] + mobility[..., 1:-1, 1:, :])
    inner = mobility[..., 1:-1, 1:-1, :]
    mean_rad = 0.5 * (inner[..., :-1] + inner[..., 1:])
    return (lat_face, lon_face, mean_rad)


def diagonal_sum(bulk, lat_face, lon_face, mean_rad):
    rad_face = radial_weight * mean_rad
    total = bulk + lat_face[..., :-1, :, :] + lat_face[..., 1:, :, :]
    total = total + lon_face[..., :, :-1, :] + lon_face[..., :, 1:, :]
    return total + pad_last(rad_face, 1, 0) + pad_last(rad_face, 0, 1)


def neighbour_total(padded, source, lat_face, lon_face, mean_rad):
    inner = padded[..., 1:-1, 1:-1, :]
    rad_face = radial_weight * mean_rad
    total = source + lat_face[..., :-1, :, :] * padded[..., :-2, 1:-1, :]
    total = total + lat_face[..., 1:, :, :] * padded[..., 2:, 1:-1, :]
    total = total + lon_face[..., :, :-1, :] * padded[..., 1:-1, :-2, :]
    total = total + lon_face[..., :, 1:, :] * padded[..., 1:-1, 2:, :]
    total = (
        total
        + pad_last(rad_face * inner[..., :-1], 1, 0)
        + pad_last(rad_face * inner[..., 1:], 0, 1)
    )
    return total


def advect(pressure_pad, porosity_pad, lat_face, lon_face, mean_rad, bulk):
    pressure_in = pressure_pad[..., 1:-1, 1:-1, :]
    porosity_in = porosity_pad[..., 2:-2, 2:-2, :]
    lat_speed = -lat_face * (pressure_pad[..., 1:, 1:-1, :] - pressure_pad[..., :-1, 1:-1, :])
    lat_left = 1.5 * porosity_pad[..., 1:-2, 2:-2, :] - 0.5 * porosity_pad[..., :-3, 2:-2, :]
    lat_right = 1.5 * porosity_pad[..., 2:-1, 2:-2, :] - 0.5 * porosity_pad[..., 3:, 2:-2, :]
    lat_flux = lat_speed * jnp.where(lat_speed > 0, lat_left, lat_right)
    lon_speed = -lon_face * (pressure_pad[..., 1:-1, 1:, :] - pressure_pad[..., 1:-1, :-1, :])
    lon_left = 1.5 * porosity_pad[..., 2:-2, 1:-2, :] - 0.5 * porosity_pad[..., 2:-2, :-3, :]
    lon_right = 1.5 * porosity_pad[..., 2:-2, 2:-1, :] - 0.5 * porosity_pad[..., 2:-2, 3:, :]
    lon_flux = lon_speed * jnp.where(lon_speed > 0, lon_left, lon_right)
    rad_speed = (
        -radial_weight * mean_rad * (pressure_in[..., 1:] - pressure_in[..., :-1])
        + buoyancy * mean_rad
    )
    rad_flux = rad_speed * jnp.where(rad_speed > 0, porosity_in[..., :-1], porosity_in[..., 1:])
    divergence = lat_flux[..., 1:, :, :] - lat_flux[..., :-1, :, :]
    divergence = divergence + lon_flux[..., :, 1:, :] - lon_flux[..., :, :-1, :]
    divergence = divergence + pad_last(rad_flux, 0, 1) - pad_last(rad_flux, 1, 0)
    return porosity_in - time_step * (divergence + bulk * pressure_in)


def body(pressure, porosity, source, bulk, lat_codes, lat_weights, lon_codes, lon_weights):
    current = pressure[0]
    porosity_now = porosity[0]
    source_now = source[0]
    bulk_now = bulk[0]
    lat_code_now = lat_codes[0]
    lat_weight_now = lat_weights[0]
    lon_code_now = lon_codes[0]
    lon_weight_now = lon_weights[0]
    levels = porosity_now.shape[-1]
    both_pad = surround(
        jnp.concatenate([porosity_now, current], axis=-1),
        2,
        lat_code_now,
        lat_weight_now,
        lon_code_now,
        lon_weight_now,
    )
    porosity_pad = both_pad[..., :levels]
    first_pad = both_pad[1:-1, 1:-1, levels:]
    near = porosity_pad[1:-1, 1:-1, :]
    mobility = near * near * near
    lat_face, lon_face, mean_rad = face_terms(mobility)
    denominator = diagonal_sum(bulk_now, lat_face, lon_face, mean_rad)
    for sweep_index in range(SWEEPS):
        if sweep_index == 0:
            padded = first_pad
        else:
            padded = surround(
                current, 1, lat_code_now, lat_weight_now, lon_code_now, lon_weight_now
            )
        current = neighbour_total(padded, source_now, lat_face, lon_face, mean_rad) / denominator
    pressure_pad = surround(current, 1, lat_code_now, lat_weight_now, lon_code_now, lon_weight_now)
    porosity_new = advect(pressure_pad, porosity_pad, lat_face, lon_face, mean_rad, bulk_now)
    return (current[None], porosity_new[None])


def solution(mesh):
    placed = (
        P("panel", "lat", "lon", None),
        P("panel", "lat", "lon", None),
        P("panel", "lat", "lon", None),
        P("panel", "lat", "lon", None),
        P("panel", None, None, "lon"),
        P("panel", None, None, None, "lon"),
        P("panel", None, None, "lat"),
        P("panel", None, None, None, "lat"),
    )
    return jax.shard_map(
        body,
        mesh=mesh,
        in_specs=placed,
        out_specs=(P("panel", "lat", "lon", None), P("panel", "lat", "lon", None)),
        check_vma=False,
    )
```

profile of v0, /device:TPU:296, one launch (start us, length us, event | category | flops | bytes accessed | tf_op | source)
XLA Modules:
  0.0 794.1 jit_solution(9546006194397543275)
XLA Ops:
  7.2 1.3 copy_bitcast_fusion
  8.6 3.4 collective-permute-start
  12.0 6.7 collective-permute-start.1
  20.1 0.9 gather_fusion.7
  21.0 0.9 gather_fusion.6
  21.9 0.9 gather_fusion.5
  22.9 0.9 gather_fusion.4
  25.6 1.3 gather_fusion.3
  26.9 1.3 gather_fusion.2
  28.2 1.3 gather_fusion.1
  29.5 1.3 gather_fusion
  33.9 1.9 collective-permute-start.2
  35.9 4.9 collective-permute-start.3
  40.7 85.8 %all-reduce.15.cloned.1.call-done = f32[2,2,16,256]{3,2,1,0:T(8,128)} async-done(((f32[2,2,16,256]{3,2,1,0:T(8,128)}), f32[2,2,16,256]{3,2,1,0:T(8,128)}) %all-reduce.15.cloned.1.call-update) | async-done | bytes 65552 | tf_op jit(solution)/shard_map/psum | solution.py:79
  126.6 174.8 %all-reduce.13.cloned.1.call-done = f32[2,2,32,256]{3,2,1,0:T(8,128)} async-done(((f32[2,2,32,256]{3,2,1,0:T(8,128)}), f32[2,2,32,256]{3,2,1,0:T(8,128)}) %all-reduce.13.cloned.1.call-update) | async-done | bytes 131088 | tf_op jit(solution)/shard_map/psum | solution.py:78
  301.3 1.0 pad_maximum_fusion.5
  302.3 3.4 collective-permute-start.4
  307.0 2.8 collective-permute-done.4
  310.2 1.9 dynamic-slice_select_fusion
  312.1 1.7 scatter.54
  316.4 6.1 collective-permute-start.6
  325.3 1.9 collective-permute-start.5
  327.3 0.9 gather_fusion.11
  330.9 82.9 %psum.58 = f32[2,1,32,128]{3,2,1,0:T(8,128)S(1)} all-reduce(f32[2,1,32,128]{3,2,1,0:T(8,128)S(1)} %multiply_add_fusion.4), channel_id=1, replica_groups=mesh['panel'=2,'lon'=16,'lat'=16] {'lat'}, use_global_device_ids=true, to_apply=%region_3.4 | all-reduce | flops 8192 | bytes 65536 | tf_op jit(solution)/shard_map/psum | solution.py:78
  413.9 45.7 %psum.59 = f32[2,1,16,128]{3,2,1,0:T(8,128)S(1)} all-reduce(f32[2,1,16,128]{3,2,1,0:T(8,128)S(1)} %multiply_add_fusion.7), channel_id=1, replica_groups=mesh['panel'=2,'lon'=16,'lat'=16] {'lon'}, use_global_device_ids=true, to_apply=%region_4.5 | all-reduce | flops 4096 | bytes 32768 | tf_op jit(solution)/shard_map/psum | solution.py:79
  459.6 2.1 collective-permute-start.7
  461.8 4.9 collective-permute-start.8
  466.6 2.4 collective-permute-start.9
  469.2 3.5 collective-permute-done.9
  472.6 1.4 scatter.60
  482.5 1.9 collective-permute-start.11
  484.5 3.9 collective-permute-start.10
  488.5 80.9 %psum.60 = f32[2,1,32,128]{3,2,1,0:T(8,128)S(1)} all-reduce(f32[2,1,32,128]{3,2,1,0:T(8,128)S(1)} %multiply_add_fusion.3), channel_id=1, replica_groups=mesh['panel'=2,'lon'=16,'lat'=16] {'lat'}, use_global_device_ids=true, to_apply=%region_5.6 | all-reduce | flops 8192 | bytes 65536 | tf_op jit(solution)/shard_map/psum | solution.py:78
  569.5 45.7 %psum.61 = f32[2,1,16,128]{3,2,1,0:T(8,128)S(1)} all-reduce(f32[2,1,16,128]{3,2,1,0:T(8,128)S(1)} %multiply_add_fusion.6), channel_id=1, replica_groups=mesh['panel'=2,'lon'=16,'lat'=16] {'lon'}, use_global_device_ids=true, to_apply=%region_6.7 | all-reduce | flops 4096 | bytes 32768 | tf_op jit(solution)/shard_map/psum | solution.py:79
  615.2 1.9 collective-permute-start.12
  617.2 4.9 collective-permute-start.13
  622.0 2.4 collective-permute-start.14
  624.6 3.5 collective-permute-done.14
  628.0 1.4 scatter.66
  638.0 1.9 collective-permute-start.16
  639.9 3.9 collective-permute-start.15
  643.9 80.9 %psum.62 = f32[2,1,32,128]{3,2,1,0:T(8,128)S(1)} all-reduce(f32[2,1,32,128]{3,2,1,0:T(8,128)S(1)} %multiply_add_fusion.2), channel_id=1, replica_groups=mesh['panel'=2,'lon'=16,'lat'=16] {'lat'}, use_global_device_ids=true, to_apply=%region_7.8 | all-reduce | flops 8192 | bytes 65536 | tf_op jit(solution)/shard_map/psum | solution.py:78
  724.9 45.7 %psum.63 = f32[2,1,16,128]{3,2,1,0:T(8,128)S(1)} all-reduce(f32[2,1,16,128]{3,2,1,0:T(8,128)S(1)} %multiply_add_fusion.5), channel_id=1, replica_groups=mesh['panel'=2,'lon'=16,'lat'=16] {'lon'}, use_global_device_ids=true, to_apply=%region_8.9 | all-reduce | flops 4096 | bytes 32768 | tf_op jit(solution)/shard_map/psum | solution.py:79
  770.7 1.9 collective-permute-start.17
  772.6 4.9 collective-permute-start.18
  777.5 2.4 collective-permute-start.19
  780.8 2.7 collective-permute-done.19
  783.4 1.4 scatter.74
  (194 shorter events, 36.7 us)
Async XLA Ops:
  7.2 119.4 %all-reduce.15.cloned.1.call-start = ((), (), s32[]{:S(2)}) async-start(), calls=%async_computation.1 | async-start | bytes 131072 | tf_op jit(solution)/shard_map/psum | solution.py:79
  8.6 25.3 %collective-permute-start = (f32[2,32,256]{2,0,1:T(2,128)S(1)}, f32[2,32,256]{2,0,1:T(2,128)S(1)}, u32[]{:S(2)}, u32[]{:S(2)}) collective-permute-start(f32[2,32,256]{2,0,1:T(2,128)S(1)} %get-tuple-element.224), channel_id=1, source_target_pairs={{0,1},{1,2},{2,3},{3,4},{4,5},{5,6},{6,7},{7,8},{8,9},{9,10},{10,1... | collective-permute-start | bytes 196616 | tf_op jit(solution)/shard_map/ppermute | solution.py:21
  12.0 21.9 %collective-permute-start.1 = (f32[2,32,256]{2,0,1:T(2,128)S(1)}, f32[2,32,256]{2,0,1:T(2,128)S(1)}, u32[]{:S(2)}, u32[]{:S(2)}) collective-permute-start(f32[2,32,256]{2,0,1:T(2,128)S(1)} %get-tuple-element.225), channel_id=1, source_target_pairs={{1,0},{2,1},{3,2},{4,3},{5,4},{6,5},{7,6},{8,7},{9,8},{10,9},{11,1... | collective-permute-start | bytes 196616 | tf_op jit(solution)/shard_map/ppermute | solution.py:23
  18.7 0.7 copy-start.6
  18.7 0.7 copy-start.4
  24.5 0.7 copy-start.7
  24.5 0.7 copy-start.5
  24.5 276.8 %all-reduce.13.cloned.1.call-start = ((), (), s32[]{:S(2)}) async-start(), calls=%async_computation | async-start | bytes 262144 | tf_op jit(solution)/shard_map/psum | solution.py:78
  31.9 0.7 copy-start.8
  33.9 273.0 %collective-permute-start.2 = (f32[20,2,256]{2,0,1:T(8,128)S(1)}, f32[20,2,256]{2,0,1:T(8,128)S(1)}, u32[]{:S(2)}, u32[]{:S(2)}) collective-permute-start(f32[20,2,256]{2,0,1:T(8,128)S(1)} %get-tuple-element.222), channel_id=1, source_target_pairs={{0,16},{16,32},{32,48},{48,64},{64,80},{80,96},{96,112},{112,128},... | collective-permute-start | bytes 122888 | tf_op jit(solution)/shard_map/ppermute | solution.py:21
  35.9 271.0 %collective-permute-start.3 = (f32[20,2,256]{2,0,1:T(8,128)S(1)}, f32[20,2,256]{2,0,1:T(8,128)S(1)}, u32[]{:S(2)}, u32[]{:S(2)}) collective-permute-start(f32[20,2,256]{2,0,1:T(8,128)S(1)} %get-tuple-element.223), channel_id=1, source_target_pairs={{16,0},{32,16},{48,32},{64,48},{80,64},{96,80},{112,96},{128,112},... | collective-permute-start | bytes 122888 | tf_op jit(solution)/shard_map/ppermute | solution.py:23
  302.3 7.6 collective-permute-start.4
  314.7 1.0 copy-start
  314.7 1.0 copy-start.1
  316.4 143.2 %collective-permute-start.6 = (f32[1,32,128]{2,0,1:T(1,128)S(1)}, f32[1,32,128]{2,0,1:T(1,128)S(1)}, u32[]{:S(2)}, u32[]{:S(2)}) collective-permute-start(f32[1,32,128]{2,0,1:T(1,128)S(1)} %slice.1083), channel_id=1, source_target_pairs={{1,0},{2,1},{3,2},{4,3},{5,4},{6,5},{7,6},{8,7},{9,8},{10,9},{11,1... | collective-permute-start | bytes 49160 | tf_op jit(solution)/shard_map/ppermute | solution.py:23
  325.3 134.3 %collective-permute-start.5 = (f32[1,32,128]{2,1,0:T(8,128)S(1)}, f32[1,32,128]{2,1,0:T(8,128)S(1)}, u32[]{:S(2)}, u32[]{:S(2)}) collective-permute-start(f32[1,32,128]{2,1,0:T(8,128)S(1)} %slice.1082), channel_id=1, source_target_pairs={{0,1},{1,2},{2,3},{3,4},{4,5},{5,6},{6,7},{7,8},{8,9},{9,10},{10,1... | collective-permute-start | bytes 49160 | tf_op jit(solution)/shard_map/ppermute | solution.py:21
  459.6 9.4 %collective-permute-start.7 = (f32[18,1,128]{2,0,1:T(8,128)S(1)}, f32[18,1,128]{2,0,1:T(8,128)S(1)}, u32[]{:S(2)}, u32[]{:S(2)}) collective-permute-start(f32[18,1,128]{2,0,1:T(8,128)S(1)} %get-tuple-element.230), channel_id=1, source_target_pairs={{0,16},{16,32},{32,48},{48,64},{64,80},{80,96},{96,112},{112,128},... | collective-permute-start | bytes 27656 | tf_op jit(solution)/shard_map/ppermute | solution.py:21
  461.8 7.3 collective-permute-start.8
  466.6 6.0 collective-permute-start.9
  474.6 1.0 copy-start.2
  482.5 132.7 %collective-permute-start.11 = (f32[1,32,128]{2,0,1:T(1,128)S(1)}, f32[1,32,128]{2,0,1:T(1,128)S(1)}, u32[]{:S(2)}, u32[]{:S(2)}) collective-permute-start(f32[1,32,128]{2,0,1:T(1,128)S(1)} %slice.1124), channel_id=1, source_target_pairs={{1,0},{2,1},{3,2},{4,3},{5,4},{6,5},{7,6},{8,7},{9,8},{10,9},{11,1... | collective-permute-start | bytes 49160 | tf_op jit(solution)/shard_map/ppermute | solution.py:23
  484.5 130.7 %collective-permute-start.10 = (f32[1,32,128]{2,1,0:T(8,128)S(1)}, f32[1,32,128]{2,1,0:T(8,128)S(1)}, u32[]{:S(2)}, u32[]{:S(2)}) collective-permute-start(f32[1,32,128]{2,1,0:T(8,128)S(1)} %slice.1123), channel_id=1, source_target_pairs={{0,1},{1,2},{2,3},{3,4},{4,5},{5,6},{6,7},{7,8},{8,9},{9,10},{10,1... | collective-permute-start | bytes 49160 | tf_op jit(solution)/shard_map/ppermute | solution.py:21
  615.2 9.2 %collective-permute-start.12 = (f32[18,1,128]{2,0,1:T(8,128)S(1)}, f32[18,1,128]{2,0,1:T(8,128)S(1)}, u32[]{:S(2)}, u32[]{:S(2)}) collective-permute-start(f32[18,1,128]{2,0,1:T(8,128)S(1)} %get-tuple-element.228), channel_id=1, source_target_pairs={{0,16},{16,32},{32,48},{48,64},{64,80},{80,96},{96,112},{112,128},... | collective-permute-start | bytes 27656 | tf_op jit(solution)/shard_map/ppermute | solution.py:21
  617.2 7.3 collective-permute-start.13
  622.0 6.0 collective-permute-start.14
  630.0 1.0 copy-start.3
  638.0 132.7 %collective-permute-start.16 = (f32[1,32,128]{2,0,1:T(1,128)S(1)}, f32[1,32,128]{2,0,1:T(1,128)S(1)}, u32[]{:S(2)}, u32[]{:S(2)}) collective-permute-start(f32[1,32,128]{2,0,1:T(1,128)S(1)} %slice.1140), channel_id=1, source_target_pairs={{1,0},{2,1},{3,2},{4,3},{5,4},{6,5},{7,6},{8,7},{9,8},{10,9},{11,1... | collective-permute-start | bytes 49160 | tf_op jit(solution)/shard_map/ppermute | solution.py:23
  639.9 130.7 %collective-permute-start.15 = (f32[1,32,128]{2,1,0:T(8,128)S(1)}, f32[1,32,128]{2,1,0:T(8,128)S(1)}, u32[]{:S(2)}, u32[]{:S(2)}) collective-permute-start(f32[1,32,128]{2,1,0:T(8,128)S(1)} %slice.1139), channel_id=1, source_target_pairs={{0,1},{1,2},{2,3},{3,4},{4,5},{5,6},{6,7},{7,8},{8,9},{9,10},{10,1... | collective-permute-start | bytes 49160 | tf_op jit(solution)/shard_map/ppermute | solution.py:21
  770.7 10.0 %collective-permute-start.17 = (f32[18,1,128]{2,0,1:T(8,128)S(1)}, f32[18,1,128]{2,0,1:T(8,128)S(1)}, u32[]{:S(2)}, u32[]{:S(2)}) collective-permute-start(f32[18,1,128]{2,0,1:T(8,128)S(1)} %get-tuple-element.226), channel_id=1, source_target_pairs={{0,16},{16,32},{32,48},{48,64},{64,80},{80,96},{96,112},{112,128},... | collective-permute-start | bytes 27656 | tf_op jit(solution)/shard_map/ppermute | solution.py:21
  772.6 8.1 %collective-permute-start.18 = (f32[18,1,128]{2,0,1:T(8,128)S(1)}, f32[18,1,128]{2,0,1:T(8,128)S(1)}, u32[]{:S(2)}, u32[]{:S(2)}) collective-permute-start(f32[18,1,128]{2,0,1:T(8,128)S(1)} %get-tuple-element.227), channel_id=1, source_target_pairs={{16,0},{32,16},{48,32},{64,48},{80,64},{96,80},{112,96},{128,112},... | collective-permute-start | bytes 27656 | tf_op jit(solution)/shard_map/ppermute | solution.py:23
  777.5 6.0 collective-permute-start.19
Sparse Core Ops, SparseCore 0:
  24.6 101.8 all-reduce.14
  130.0 171.2 all-reduce.12
where the time goes:
time: 795 us; the launch traced here: 794 us
  blocking collectives  382 us (48%)
  waiting for transfers between devices  273 us (34%)
  starting transfers between devices  67.7 us (9%)
  local copies, waits for them, and re-layouts  46.2 us (6%)
  between operations  15.1 us (2%)
  other arithmetic  10.1 us (1%)
    psum x3, blocking collectives, surround(): lat_summed = lax.psum(lat_terms, 'lat')  245 us
    psum x1, waiting for transfers between devices, surround(): lat_summed = lax.psum(lat_terms, 'lat')  175 us
    psum x3, blocking collectives, surround(): lon_summed = lax.psum(lon_terms, 'lon')  137 us
    psum x1, waiting for transfers between devices, surround(): lon_summed = lax.psum(lon_terms, 'lon')  85.8 us
    ppermute x8, starting transfers between devices, padded_2(): lax.ppermute(head, axis, [((i + 1) % count, i) for i in range(ends)])  36 us
    ppermute x8, starting transfers between devices, padded_2(): lax.ppermute(tail, axis, [(i, (i + 1) % count) for i in range(ends)])  21 us
  transfers between devices with their start and end apart: 22, of which 6 were waited for; matrix products, arithmetic and copies ran while one was open for 3% of the time, Pallas kernels for 0%

commit v1 on v0

--- a/solution.py
+++ b/solution.py
@@ -1,3 +1,4 @@
+import functools
 import jax
 import jax.numpy as jnp
 from jax import lax
@@ -8,6 +9,23 @@
 radial_weight = 0.25
 buoyancy = 0.5
 time_step = 0.04
+
+
+def form_quotas(tile_in, chip_axis):
+    chips = jax.lax.axis_size(chip_axis)
+    new, x_next = (tile_in, 0)
+    while 1 << x_next < chips:
+        r1 = jax.lax.ppermute(
+            new,
+            axis_name=chip_axis,
+            perm=tuple(((dev_j, dev_j ^ 1 << x_next) for dev_j in range(chips))),
+        )
+        new = new + r1
+        x_next = x_next + 1
+    return new
+
+
+find_squares_for = functools.partial(form_quotas, chip_axis="lon")
 
 
 def padded_2(cells, sides, width):
@@ -76,7 +94,7 @@
     padded = padded_2(field, (("lat", 0), ("lon", 1)), width)
     lat_terms, lon_terms = rim_terms(field, lat_codes, lat_weights, lon_codes, lon_weights, width)
     lat_summed = lax.psum(lat_terms, "lat")
-    lon_summed = lax.psum(lon_terms, "lon")
+    lon_summed = find_squares_for(lon_terms)
     arrived = swapped(jnp.concatenate([lat_summed, lon_summed], axis=2), "panel", 0)
     lat_rim = arrived[:, :, :cols_dev]
     lon_rim = arrived[:, :, cols_dev:]

time: 795 us -> 608 us (0.76)
  the two profiles are of different devices: /device:TPU:296 before, /device:TPU:168 now
where the time goes in v1:
time: 608 us; the launch traced here: 606 us
  blocking collectives  245 us (40%)
  waiting for transfers between devices  170 us (28%)
  starting transfers between devices  122 us (20%)
  local copies, waits for them, and re-layouts  44.7 us (7%)
  between operations  15.5 us (3%)
  other arithmetic  9.69 us (2%)
    psum x3, blocking collectives, surround(): lat_summed = lax.psum(lat_terms, 'lat')  245 us
    psum x1, waiting for transfers between devices, surround(): lat_summed = lax.psum(lat_terms, 'lat')  141 us
    ppermute x16, starting transfers between devices, form_quotas(): jax.lax.ppermute(new, axis_name=chip_axis, perm=tuple(((dev_j, dev_j ^ 1...  59.1 us
    ppermute x8, starting transfers between devices, padded_2(): lax.ppermute(head, axis, [((i + 1) % count, i) for i in range(ends)])  31.1 us
    ppermute x8, starting transfers between devices, padded_2(): lax.ppermute(tail, axis, [(i, (i + 1) % count) for i in range(ends)])  20.8 us
    gather x16, local copies, waits for them, and re-layouts, rim_terms(): picked = field[jnp.clip(target, 0, rows_dev - 1), cols_at + col_step]  15.7 us
    ppermute x16, waiting for transfers between devices, form_quotas(): jax.lax.ppermute(new, axis_name=chip_axis, perm=tuple(((dev_j, dev_j ^ 1...  14.8 us
    ppermute x4, waiting for transfers between devices, swapped(): return lax.ppermute(block, axis, route)  13.5 us
  transfers between devices with their start and end apart: 37, of which 10 were waited for; matrix products, arithmetic and copies ran while one was open for 4% of the time, Pallas kernels for 0%

profile of v1, /device:TPU:168, one launch (start us, length us, event | category | flops | bytes accessed | tf_op | source)
XLA Modules:
  0.0 606.2 jit_solution(17670497854500235593)
XLA Ops:
  8.6 3.4 collective-permute-start
  12.0 6.7 %collective-permute-start.1 = (f32[2,32,256]{2,0,1:T(2,128)S(1)}, f32[2,32,256]{2,0,1:T(2,128)S(1)}, u32[]{:S(2)}, u32[]{:S(2)}) collective-permute-start(f32[2,32,256]{2,0,1:T(2,128)S(1)} %get-tuple-element.225), channel_id=1, source_target_pairs={{1,0},{2,1},{3,2},{4,3},{5,4},{6,5},{7,6},{8,7},{9,8},{10,9},{11,1... | collective-permute-start | bytes 196616 | tf_op jit(solution)/shard_map/ppermute | solution.py:41
  23.9 1.9 collective-permute-start.4
  32.6 4.3 collective-permute-start.5
  37.0 2.7 collective-permute-done.5
  39.7 1.9 collective-permute-start.6
  42.4 4.4 collective-permute-done.6
  46.8 8.6 %collective-permute-start.7 = (f32[2,2,16,256]{3,2,1,0:T(8,128)S(1)}, f32[2,2,16,256]{3,2,1,0:T(8,128)S(1)}, u32[]{:S(2)}, u32[]{:S(2)}) collective-permute-start(f32[2,2,16,256]{3,2,1,0:T(8,128)S(1)} %add.807), channel_id=1, source_target_pairs={{0,128},{16,144},{32,160},{48,176},{64,192},{80,208},{96,224},{112... | collective-permute-start | bytes 196616 | tf_op jit(solution)/shard_map/ppermute | solution.py:18
  55.4 1.9 collective-permute-start.2
  57.3 3.6 collective-permute-start.3
  61.0 141.4 %all-reduce.12.cloned.1.call-done = f32[2,2,32,256]{3,2,1,0:T(8,128)} async-done(((f32[2,2,32,256]{3,2,1,0:T(8,128)}), f32[2,2,32,256]{3,2,1,0:T(8,128)}) %all-reduce.12.cloned.1.call-update) | async-done | bytes 131088 | tf_op jit(solution)/shard_map/psum | solution.py:96
  203.3 3.4 collective-permute-start.8
  207.8 3.2 collective-permute-done.8
  211.2 2.0 dynamic-slice_select_fusion
  220.4 1.9 collective-permute-start.13
  223.3 6.1 %collective-permute-start.10 = (f32[1,32,128]{2,0,1:T(1,128)S(1)}, f32[1,32,128]{2,0,1:T(1,128)S(1)}, u32[]{:S(2)}, u32[]{:S(2)}) collective-permute-start(f32[1,32,128]{2,0,1:T(1,128)S(1)} %slice.1083), channel_id=1, source_target_pairs={{1,0},{2,1},{3,2},{4,3},{5,4},{6,5},{7,6},{8,7},{9,8},{10,9},{11,1... | collective-permute-start | bytes 49160 | tf_op jit(solution)/shard_map/ppermute | solution.py:41
  229.4 1.9 collective-permute-start.9
  234.9 3.6 collective-permute-start.14
  238.5 2.0 collective-permute-done.14
  240.5 2.1 collective-permute-start.15
  242.6 82.9 %psum.29 = f32[2,1,32,128]{3,2,1,0:T(8,128)S(1)} all-reduce(f32[2,1,32,128]{3,2,1,0:T(8,128)S(1)} %multiply_add_fusion.4), channel_id=1, replica_groups=mesh['panel'=2,'lon'=16,'lat'=16] {'lat'}, use_global_device_ids=true, to_apply=%region_2.3 | all-reduce | flops 8192 | bytes 65536 | tf_op jit(solution)/shard_map/psum | solution.py:96
  325.5 8.1 %collective-permute-start.16 = (f32[2,1,16,128]{3,2,1,0:T(8,128)S(1)}, f32[2,1,16,128]{3,2,1,0:T(8,128)S(1)}, u32[]{:S(2)}, u32[]{:S(2)}) collective-permute-start(f32[2,1,16,128]{3,2,1,0:T(8,128)S(1)} %add.848), channel_id=1, source_target_pairs={{0,128},{16,144},{32,160},{48,176},{64,192},{80,208},{96,224},{112... | collective-permute-start | bytes 49160 | tf_op jit(solution)/shard_map/ppermute | solution.py:18
  333.6 1.9 collective-permute-start.11
  335.5 3.6 collective-permute-start.12
  339.2 2.4 collective-permute-start.17
  341.8 3.5 collective-permute-done.17
  351.6 1.9 collective-permute-start.22
  357.1 1.9 collective-permute-start.19
  359.0 3.9 collective-permute-start.18
  363.0 2.7 collective-permute-start.23
  365.7 2.9 collective-permute-done.23
  370.5 80.9 %psum.30 = f32[2,1,32,128]{3,2,1,0:T(8,128)S(1)} all-reduce(f32[2,1,32,128]{3,2,1,0:T(8,128)S(1)} %multiply_add_fusion.3), channel_id=1, replica_groups=mesh['panel'=2,'lon'=16,'lat'=16] {'lat'}, use_global_device_ids=true, to_apply=%region_3.4 | all-reduce | flops 8192 | bytes 65536 | tf_op jit(solution)/shard_map/psum | solution.py:96
  451.5 5.6 collective-permute-start.25
  457.1 1.9 collective-permute-start.20
  459.1 3.6 collective-permute-start.21
  462.7 2.4 collective-permute-start.26
  465.3 3.5 collective-permute-done.26
  475.1 1.9 collective-permute-start.31
  480.6 1.9 collective-permute-start.28
  482.5 3.9 collective-permute-start.27
  486.5 2.7 collective-permute-start.32
  489.3 2.8 collective-permute-done.32
  492.1 3.0 collective-permute-start.33
  495.2 80.9 %psum.31 = f32[2,1,32,128]{3,2,1,0:T(8,128)S(1)} all-reduce(f32[2,1,32,128]{3,2,1,0:T(8,128)S(1)} %multiply_add_fusion.2), channel_id=1, replica_groups=mesh['panel'=2,'lon'=16,'lat'=16] {'lat'}, use_global_device_ids=true, to_apply=%region_4.5 | all-reduce | flops 8192 | bytes 65536 | tf_op jit(solution)/shard_map/psum | solution.py:96
  576.8 7.1 %collective-permute-start.34 = (f32[2,1,16,128]{3,2,1,0:T(8,128)S(1)}, f32[2,1,16,128]{3,2,1,0:T(8,128)S(1)}, u32[]{:S(2)}, u32[]{:S(2)}) collective-permute-start(f32[2,1,16,128]{3,2,1,0:T(8,128)S(1)} %add.880), channel_id=1, source_target_pairs={{0,128},{16,144},{32,160},{48,176},{64,192},{80,208},{96,224},{112... | collective-permute-start | bytes 49160 | tf_op jit(solution)/shard_map/ppermute | solution.py:18
  585.9 3.6 collective-permute-start.30
  589.6 2.4 collective-permute-start.35
  592.1 3.5 collective-permute-done.35
  (236 shorter events, 56.4 us)
Async XLA Ops:
  7.2 195.3 %all-reduce.12.cloned.1.call-start = ((), (), s32[]{:S(2)}) async-start(), calls=%async_computation | async-start | bytes 262144 | tf_op jit(solution)/shard_map/psum | solution.py:96
  8.6 46.7 %collective-permute-start = (f32[2,32,256]{2,0,1:T(2,128)S(1)}, f32[2,32,256]{2,0,1:T(2,128)S(1)}, u32[]{:S(2)}, u32[]{:S(2)}) collective-permute-start(f32[2,32,256]{2,0,1:T(2,128)S(1)} %get-tuple-element.224), channel_id=1, source_target_pairs={{0,1},{1,2},{2,3},{3,4},{4,5},{5,6},{6,7},{7,8},{8,9},{9,10},{10,1... | collective-permute-start | bytes 196616 | tf_op jit(solution)/shard_map/ppermute | solution.py:39
  12.0 43.3 %collective-permute-start.1 = (f32[2,32,256]{2,0,1:T(2,128)S(1)}, f32[2,32,256]{2,0,1:T(2,128)S(1)}, u32[]{:S(2)}, u32[]{:S(2)}) collective-permute-start(f32[2,32,256]{2,0,1:T(2,128)S(1)} %get-tuple-element.225), channel_id=1, source_target_pairs={{1,0},{2,1},{3,2},{4,3},{5,4},{6,5},{7,6},{8,7},{9,8},{10,9},{11,1... | collective-permute-start | bytes 196616 | tf_op jit(solution)/shard_map/ppermute | solution.py:41
  18.7 0.7 copy-start.6
  18.7 0.7 copy-start.4
  23.8 2.1 copy-start.7
  23.9 2.0 copy-start.5
  23.9 8.7 %collective-permute-start.4 = (f32[2,2,16,256]{3,2,1,0:T(8,128)S(1)}, f32[2,2,16,256]{3,2,1,0:T(8,128)S(1)}, u32[]{:S(2)}, u32[]{:S(2)}) collective-permute-start(f32[2,2,16,256]{3,2,1,0:T(8,128)S(1)} %multiply_add_fusion.1), channel_id=1, source_target_pairs={{0,16},{16,0},{32,48},{48,32},{64,80},{80,64},{96,112},{112,96},{1... | collective-permute-start | bytes 196616 | tf_op jit(solution)/shard_map/ppermute | solution.py:18
  32.6 7.0 %collective-permute-start.5 = (f32[2,2,16,256]{3,2,1,0:T(8,128)S(1)}, f32[2,2,16,256]{3,2,1,0:T(8,128)S(1)}, u32[]{:S(2)}, u32[]{:S(2)}) collective-permute-start(f32[2,2,16,256]{3,2,1,0:T(8,128)S(1)} %add.805), channel_id=1, source_target_pairs={{0,32},{16,48},{32,0},{48,16},{64,96},{80,112},{96,64},{112,80},{1... | collective-permute-start | bytes 196616 | tf_op jit(solution)/shard_map/ppermute | solution.py:18
  36.9 4.7 copy-start.8
  39.7 7.1 %collective-permute-start.6 = (f32[2,2,16,256]{3,2,1,0:T(8,128)S(1)}, f32[2,2,16,256]{3,2,1,0:T(8,128)S(1)}, u32[]{:S(2)}, u32[]{:S(2)}) collective-permute-start(f32[2,2,16,256]{3,2,1,0:T(8,128)S(1)} %add.806), channel_id=1, source_target_pairs={{0,64},{16,80},{32,96},{48,112},{64,0},{80,16},{96,32},{112,48},{1... | collective-permute-start | bytes 196616 | tf_op jit(solution)/shard_map/ppermute | solution.py:18
  46.8 14.2 %collective-permute-start.7 = (f32[2,2,16,256]{3,2,1,0:T(8,128)S(1)}, f32[2,2,16,256]{3,2,1,0:T(8,128)S(1)}, u32[]{:S(2)}, u32[]{:S(2)}) collective-permute-start(f32[2,2,16,256]{3,2,1,0:T(8,128)S(1)} %add.807), channel_id=1, source_target_pairs={{0,128},{16,144},{32,160},{48,176},{64,192},{80,208},{96,224},{112... | collective-permute-start | bytes 196616 | tf_op jit(solution)/shard_map/ppermute | solution.py:18
  55.4 152.2 %collective-permute-start.2 = (f32[20,2,256]{2,0,1:T(8,128)S(1)}, f32[20,2,256]{2,0,1:T(8,128)S(1)}, u32[]{:S(2)}, u32[]{:S(2)}) collective-permute-start(f32[20,2,256]{2,0,1:T(8,128)S(1)} %get-tuple-element.222), channel_id=1, source_target_pairs={{0,16},{16,32},{32,48},{48,64},{64,80},{80,96},{96,112},{112,128},... | collective-permute-start | bytes 122888 | tf_op jit(solution)/shard_map/ppermute | solution.py:39
  57.3 150.3 %collective-permute-start.3 = (f32[20,2,256]{2,0,1:T(8,128)S(1)}, f32[20,2,256]{2,0,1:T(8,128)S(1)}, u32[]{:S(2)}, u32[]{:S(2)}) collective-permute-start(f32[20,2,256]{2,0,1:T(8,128)S(1)} %get-tuple-element.223), channel_id=1, source_target_pairs={{16,0},{32,16},{48,32},{64,48},{80,64},{96,80},{112,96},{128,112},... | collective-permute-start | bytes 122888 | tf_op jit(solution)/shard_map/ppermute | solution.py:41
  203.3 7.6 %collective-permute-start.8 = (f32[2,2,48,256]{3,2,1,0:T(8,128)S(1)}, f32[2,2,48,256]{3,2,1,0:T(8,128)S(1)}, u32[]{:S(2)}, u32[]{:S(2)}) collective-permute-start(f32[2,2,48,256]{3,2,1,0:T(8,128)S(1)} %pad_maximum_fusion.5), channel_id=1, source_target_pairs={{0,256},{256,0},{1,257},{257,1},{2,258},{258,2},{3,259},{259,3},{4... | collective-permute-start | bytes 589832 | tf_op jit(solution)/shard_map/ppermute | solution.py:55
  215.8 1.0 copy-start
  215.8 1.0 copy-start.1
  220.4 14.4 %collective-permute-start.13 = (f32[2,1,16,128]{3,2,1,0:T(8,128)S(1)}, f32[2,1,16,128]{3,2,1,0:T(8,128)S(1)}, u32[]{:S(2)}, u32[]{:S(2)}) collective-permute-start(f32[2,1,16,128]{3,2,1,0:T(8,128)S(1)} %multiply_add_fusion.7), channel_id=1, source_target_pairs={{0,16},{16,0},{32,48},{48,32},{64,80},{80,64},{96,112},{112,96},{1... | collective-permute-start | bytes 49160 | tf_op jit(solution)/shard_map/ppermute | solution.py:18
  223.3 110.3 %collective-permute-start.10 = (f32[1,32,128]{2,0,1:T(1,128)S(1)}, f32[1,32,128]{2,0,1:T(1,128)S(1)}, u32[]{:S(2)}, u32[]{:S(2)}) collective-permute-start(f32[1,32,128]{2,0,1:T(1,128)S(1)} %slice.1083), channel_id=1, source_target_pairs={{1,0},{2,1},{3,2},{4,3},{5,4},{6,5},{7,6},{8,7},{9,8},{10,9},{11,1... | collective-permute-start | bytes 49160 | tf_op jit(solution)/shard_map/ppermute | solution.py:41
  229.4 104.2 %collective-permute-start.9 = (f32[1,32,128]{2,1,0:T(8,128)S(1)}, f32[1,32,128]{2,1,0:T(8,128)S(1)}, u32[]{:S(2)}, u32[]{:S(2)}) collective-permute-start(f32[1,32,128]{2,1,0:T(8,128)S(1)} %slice.1082), channel_id=1, source_target_pairs={{0,1},{1,2},{2,3},{3,4},{4,5},{5,6},{6,7},{7,8},{8,9},{9,10},{10,1... | collective-permute-start | bytes 49160 | tf_op jit(solution)/shard_map/ppermute | solution.py:39
  234.9 5.6 collective-permute-start.14
  240.5 85.0 %collective-permute-start.15 = (f32[2,1,16,128]{3,2,1,0:T(8,128)S(1)}, f32[2,1,16,128]{3,2,1,0:T(8,128)S(1)}, u32[]{:S(2)}, u32[]{:S(2)}) collective-permute-start(f32[2,1,16,128]{3,2,1,0:T(8,128)S(1)} %add.847), channel_id=1, source_target_pairs={{0,64},{16,80},{32,96},{48,112},{64,0},{80,16},{96,32},{112,48},{1... | collective-permute-start | bytes 49160 | tf_op jit(solution)/shard_map/ppermute | solution.py:18
  325.5 13.7 %collective-permute-start.16 = (f32[2,1,16,128]{3,2,1,0:T(8,128)S(1)}, f32[2,1,16,128]{3,2,1,0:T(8,128)S(1)}, u32[]{:S(2)}, u32[]{:S(2)}) collective-permute-start(f32[2,1,16,128]{3,2,1,0:T(8,128)S(1)} %add.848), channel_id=1, source_target_pairs={{0,128},{16,144},{32,160},{48,176},{64,192},{80,208},{96,224},{112... | collective-permute-start | bytes 49160 | tf_op jit(solution)/shard_map/ppermute | solution.py:18
  333.6 8.1 %collective-permute-start.11 = (f32[18,1,128]{2,0,1:T(8,128)S(1)}, f32[18,1,128]{2,0,1:T(8,128)S(1)}, u32[]{:S(2)}, u32[]{:S(2)}) collective-permute-start(f32[18,1,128]{2,0,1:T(8,128)S(1)} %get-tuple-element.230), channel_id=1, source_target_pairs={{0,16},{16,32},{32,48},{48,64},{64,80},{80,96},{96,112},{112,128},... | collective-permute-start | bytes 27656 | tf_op jit(solution)/shard_map/ppermute | solution.py:39
  335.5 6.1 %collective-permute-start.12 = (f32[18,1,128]{2,0,1:T(8,128)S(1)}, f32[18,1,128]{2,0,1:T(8,128)S(1)}, u32[]{:S(2)}, u32[]{:S(2)}) collective-permute-start(f32[18,1,128]{2,0,1:T(8,128)S(1)} %get-tuple-element.231), channel_id=1, source_target_pairs={{16,0},{32,16},{48,32},{64,48},{80,64},{96,80},{112,96},{128,112},... | collective-permute-start | bytes 27656 | tf_op jit(solution)/shard_map/ppermute | solution.py:41
  339.2 6.0 collective-permute-start.17
  347.1 1.0 copy-start.2
  351.6 11.4 %collective-permute-start.22 = (f32[2,1,16,128]{3,2,1,0:T(8,128)S(1)}, f32[2,1,16,128]{3,2,1,0:T(8,128)S(1)}, u32[]{:S(2)}, u32[]{:S(2)}) collective-permute-start(f32[2,1,16,128]{3,2,1,0:T(8,128)S(1)} %multiply_add_fusion.6), channel_id=1, source_target_pairs={{0,16},{16,0},{32,48},{48,32},{64,80},{80,64},{96,112},{112,96},{1... | collective-permute-start | bytes 49160 | tf_op jit(solution)/shard_map/ppermute | solution.py:18
  357.1 100.0 %collective-permute-start.19 = (f32[1,32,128]{2,0,1:T(1,128)S(1)}, f32[1,32,128]{2,0,1:T(1,128)S(1)}, u32[]{:S(2)}, u32[]{:S(2)}) collective-permute-start(f32[1,32,128]{2,0,1:T(1,128)S(1)} %slice.1124), channel_id=1, source_target_pairs={{1,0},{2,1},{3,2},{4,3},{5,4},{6,5},{7,6},{8,7},{9,8},{10,9},{11,1... | collective-permute-start | bytes 49160 | tf_op jit(solution)/shard_map/ppermute | solution.py:41
  359.0 98.1 %collective-permute-start.18 = (f32[1,32,128]{2,1,0:T(8,128)S(1)}, f32[1,32,128]{2,1,0:T(8,128)S(1)}, u32[]{:S(2)}, u32[]{:S(2)}) collective-permute-start(f32[1,32,128]{2,1,0:T(8,128)S(1)} %slice.1123), channel_id=1, source_target_pairs={{0,1},{1,2},{2,3},{3,4},{4,5},{5,6},{6,7},{7,8},{8,9},{9,10},{10,1... | collective-permute-start | bytes 49160 | tf_op jit(solution)/shard_map/ppermute | solution.py:39
  363.0 5.6 collective-permute-start.23
  368.6 82.9 %collective-permute-start.24 = (f32[2,1,16,128]{3,2,1,0:T(8,128)S(1)}, f32[2,1,16,128]{3,2,1,0:T(8,128)S(1)}, u32[]{:S(2)}, u32[]{:S(2)}) collective-permute-start(f32[2,1,16,128]{3,2,1,0:T(8,128)S(1)} %add.863), channel_id=1, source_target_pairs={{0,64},{16,80},{32,96},{48,112},{64,0},{80,16},{96,32},{112,48},{1... | collective-permute-start | bytes 49160 | tf_op jit(solution)/shard_map/ppermute | solution.py:18
  451.5 11.2 %collective-permute-start.25 = (f32[2,1,16,128]{3,2,1,0:T(8,128)S(1)}, f32[2,1,16,128]{3,2,1,0:T(8,128)S(1)}, u32[]{:S(2)}, u32[]{:S(2)}) collective-permute-start(f32[2,1,16,128]{3,2,1,0:T(8,128)S(1)} %add.864), channel_id=1, source_target_pairs={{0,128},{16,144},{32,160},{48,176},{64,192},{80,208},{96,224},{112... | collective-permute-start | bytes 49160 | tf_op jit(solution)/shard_map/ppermute | solution.py:18
  457.1 8.1 %collective-permute-start.20 = (f32[18,1,128]{2,0,1:T(8,128)S(1)}, f32[18,1,128]{2,0,1:T(8,128)S(1)}, u32[]{:S(2)}, u32[]{:S(2)}) collective-permute-start(f32[18,1,128]{2,0,1:T(8,128)S(1)} %get-tuple-element.228), channel_id=1, source_target_pairs={{0,16},{16,32},{32,48},{48,64},{64,80},{80,96},{96,112},{112,128},... | collective-permute-start | bytes 27656 | tf_op jit(solution)/shard_map/ppermute | solution.py:39
  459.1 6.1 %collective-permute-start.21 = (f32[18,1,128]{2,0,1:T(8,128)S(1)}, f32[18,1,128]{2,0,1:T(8,128)S(1)}, u32[]{:S(2)}, u32[]{:S(2)}) collective-permute-start(f32[18,1,128]{2,0,1:T(8,128)S(1)} %get-tuple-element.229), channel_id=1, source_target_pairs={{16,0},{32,16},{48,32},{64,48},{80,64},{96,80},{112,96},{128,112},... | collective-permute-start | bytes 27656 | tf_op jit(solution)/shard_map/ppermute | solution.py:41
  462.7 6.0 collective-permute-start.26
  470.6 1.0 copy-start.3
  475.1 11.4 %collective-permute-start.31 = (f32[2,1,16,128]{3,2,1,0:T(8,128)S(1)}, f32[2,1,16,128]{3,2,1,0:T(8,128)S(1)}, u32[]{:S(2)}, u32[]{:S(2)}) collective-permute-start(f32[2,1,16,128]{3,2,1,0:T(8,128)S(1)} %multiply_add_fusion.5), channel_id=1, source_target_pairs={{0,16},{16,0},{32,48},{48,32},{64,80},{80,64},{96,112},{112,96},{1... | collective-permute-start | bytes 49160 | tf_op jit(solution)/shard_map/ppermute | solution.py:18
  480.6 103.3 %collective-permute-start.28 = (f32[1,32,128]{2,0,1:T(1,128)S(1)}, f32[1,32,128]{2,0,1:T(1,128)S(1)}, u32[]{:S(2)}, u32[]{:S(2)}) collective-permute-start(f32[1,32,128]{2,0,1:T(1,128)S(1)} %slice.1140), channel_id=1, source_target_pairs={{1,0},{2,1},{3,2},{4,3},{5,4},{6,5},{7,6},{8,7},{9,8},{10,9},{11,1... | collective-permute-start | bytes 49160 | tf_op jit(solution)/shard_map/ppermute | solution.py:41
  482.5 101.4 %collective-permute-start.27 = (f32[1,32,128]{2,1,0:T(8,128)S(1)}, f32[1,32,128]{2,1,0:T(8,128)S(1)}, u32[]{:S(2)}, u32[]{:S(2)}) collective-permute-start(f32[1,32,128]{2,1,0:T(8,128)S(1)} %slice.1139), channel_id=1, source_target_pairs={{0,1},{1,2},{2,3},{3,4},{4,5},{5,6},{6,7},{7,8},{8,9},{9,10},{10,1... | collective-permute-start | bytes 49160 | tf_op jit(solution)/shard_map/ppermute | solution.py:39
  486.5 5.6 collective-permute-start.32
  492.1 84.7 %collective-permute-start.33 = (f32[2,1,16,128]{3,2,1,0:T(8,128)S(1)}, f32[2,1,16,128]{3,2,1,0:T(8,128)S(1)}, u32[]{:S(2)}, u32[]{:S(2)}) collective-permute-start(f32[2,1,16,128]{3,2,1,0:T(8,128)S(1)} %add.879), channel_id=1, source_target_pairs={{0,64},{16,80},{32,96},{48,112},{64,0},{80,16},{96,32},{112,48},{1... | collective-permute-start | bytes 49160 | tf_op jit(solution)/shard_map/ppermute | solution.py:18
  576.8 12.7 %collective-permute-start.34 = (f32[2,1,16,128]{3,2,1,0:T(8,128)S(1)}, f32[2,1,16,128]{3,2,1,0:T(8,128)S(1)}, u32[]{:S(2)}, u32[]{:S(2)}) collective-permute-start(f32[2,1,16,128]{3,2,1,0:T(8,128)S(1)} %add.880), channel_id=1, source_target_pairs={{0,128},{16,144},{32,160},{48,176},{64,192},{80,208},{96,224},{112... | collective-permute-start | bytes 49160 | tf_op jit(solution)/shard_map/ppermute | solution.py:18
  584.0 8.1 %collective-permute-start.29 = (f32[18,1,128]{2,0,1:T(8,128)S(1)}, f32[18,1,128]{2,0,1:T(8,128)S(1)}, u32[]{:S(2)}, u32[]{:S(2)}) collective-permute-start(f32[18,1,128]{2,0,1:T(8,128)S(1)} %get-tuple-element.226), channel_id=1, source_target_pairs={{0,16},{16,32},{32,48},{48,64},{64,80},{80,96},{96,112},{112,128},... | collective-permute-start | bytes 27656 | tf_op jit(solution)/shard_map/ppermute | solution.py:39
  585.9 6.1 %collective-permute-start.30 = (f32[18,1,128]{2,0,1:T(8,128)S(1)}, f32[18,1,128]{2,0,1:T(8,128)S(1)}, u32[]{:S(2)}, u32[]{:S(2)}) collective-permute-start(f32[18,1,128]{2,0,1:T(8,128)S(1)} %get-tuple-element.227), channel_id=1, source_target_pairs={{16,0},{32,16},{48,32},{64,48},{80,64},{96,80},{112,96},{128,112},... | collective-permute-start | bytes 27656 | tf_op jit(solution)/shard_map/ppermute | solution.py:41
  589.6 6.0 collective-permute-start.35
Sparse Core Ops, SparseCore 0:
  32.3 170.0 all-reduce.11
